TPU v7x, 256 devices: a whole 4x4x8 slice. The times are simulated.
256 devices in a mesh: seq: 64 (over z_lo, y, x, core), chan: 4 (over z_hi).
Axes of the slice: x: 4, y: 4, z: 8 (z_hi: 4, z_lo: 2; z = z_hi * 2 + z_lo), core: 2. Of those that a mesh axis runs over, the one named last changes fastest.
Arguments:
- features: bfloat16 [3, 2, 8192, 8192], P(None, None, 'chan', 'seq'), may hold values from -6 to 6
- offsets: int32 [2], replicated, may hold values from 0 to 4095
- tokens: int32 [2, 4], replicated, may hold values from 0 to 511
- decay_rate: float32 [16, 8192], P(None, 'chan'), may hold values from 0 to 1
- residue: float32 [16, 8192], P(None, 'chan'), may hold values from -1 to 1
- skip_weight: float32 [8192], P('chan'), may hold values from -3 to 3
- embedding: bfloat16 [512, 8192], P(None, 'seq'), may hold values from -12 to 12
- norm_gain: float32 [8192], P('seq'), may hold values from 0.1 to 1.9
- dec_weight: bfloat16 [3, 8192, 8192], P(None, 'seq', 'chan'), may hold values from -0.1875 to 0.1875
- out_weight: bfloat16 [8192, 8192], P('chan', 'seq'), may hold values from -0.1875 to 0.1875
Outputs:
- mixed: bfloat16 [2, 8192, 8192], P(None, 'chan', 'seq')
- decoded: bfloat16 [2, 4, 8192], P(None, None, ('seq', 'chan'))
All inputs are finite; a program needn't handle non-finite values.
Results may differ from a plain program's by a relative error of at most 0.0082.
Values may be sent and summed in bfloat16 or wider, within the bound.
No kernel may reach another device: no remote copies, remote signals or barrier semaphores. Data moves between devices by JAX's collectives and lax.ppermute only.
A program may use at most 128 MiB of HBM per device.

v0:
```python
import math
import jax
import jax.numpy as jnp
from jax import lax
from jax.sharding import PartitionSpec as P

D = 8192
highest = lax.Precision.HIGHEST


def local_conv(signal, rates, residues, skips, start_state):
    batch_rows, channels, length = signal.shape
    modes = rates.shape[0]
    block = math.gcd(length, 256)
    blocks = length // block
    group = math.gcd(channels, max(1, 2**21 // (block * block)))
    groups = channels // group

    def one_group(packed):
        sig_group, rate_group, res_group, skip_group, start_group = packed
        expo = -rate_group
        lag_pos = jnp.arange(block, dtype=jnp.float32)
        filt = jnp.sum(res_group[:, :, None] * jnp.exp(expo[:, :, None] * lag_pos), axis=0)
        distance = jnp.arange(block)[:, None] - jnp.arange(block)[None, :]
        toeplitz = jnp.where(distance >= 0, jnp.take(filt, jnp.maximum(distance, 0), axis=1), 0.0)
        blocked = sig_group.reshape(batch_rows, group, blocks, block)
        inner = jnp.einsum("gij,bgnj->bgni", toeplitz, blocked, precision=highest)
        tail_weight = jnp.exp(expo[:, :, None] * (block - 1.0 - lag_pos))
        block_sums = jnp.einsum("mgj,bgnj->bmgn", tail_weight, blocked, precision=highest)
        block_pos = jnp.arange(blocks, dtype=jnp.float32)
        block_gap = block_pos[:, None] - 1.0 - block_pos[None, :]
        spread = jnp.where(
            block_gap >= 0,
            jnp.exp(expo[:, :, None, None] * block * jnp.maximum(block_gap, 0.0)),
            0.0,
        )
        carried = jnp.einsum("mgnk,bmgk->bmgn", spread, block_sums, precision=highest)
        carried = (
            carried + jnp.exp(expo[:, :, None] * block * block_pos)[None] * start_group[..., None]
        )
        head_weight = res_group[:, :, None] * jnp.exp(expo[:, :, None] * (lag_pos + 1.0))
        outer = jnp.einsum("mgi,bmgn->bgni", head_weight, carried, precision=highest)
        conv = (inner + outer).reshape(batch_rows, group, length) + skip_group[
            None, :, None
        ] * sig_group
        final = jnp.exp(expo * block)[None] * carried[..., -1] + block_sums[..., -1]
        return (conv, final)

    packed = (
        signal.reshape(batch_rows, groups, group, length).transpose(1, 0, 2, 3),
        rates.reshape(modes, groups, group).transpose(1, 0, 2),
        residues.reshape(modes, groups, group).transpose(1, 0, 2),
        skips.reshape(groups, group),
        start_state.reshape(batch_rows, modes, groups, group).transpose(2, 0, 1, 3),
    )
    conv, final = lax.map(one_group, packed)
    conv = conv.transpose(1, 0, 2, 3).reshape(batch_rows, channels, length)
    final = final.transpose(1, 2, 0, 3).reshape(batch_rows, modes, channels)
    return (conv, final)


def body(
    features,
    offsets,
    tokens,
    decay_rate,
    residue,
    skip_weight,
    embedding,
    norm_gain,
    dec_weight,
    out_weight,
):
    seq_count = lax.axis_size("seq")
    seq_index = lax.axis_index("seq")
    query = features[0]
    keys_in = features[1]
    values_in = features[2]
    batch_rows, local_chans, shard_len = query.shape
    modes = decay_rate.shape[0]
    positions = seq_index * shard_len + jnp.arange(shard_len, dtype=jnp.int32)
    live = positions[None, :] >= offsets[:, None]
    product = jnp.where(
        live[:, None, :], keys_in.astype(jnp.float32) * values_in.astype(jnp.float32), 0.0
    ).astype(jnp.bfloat16)
    per_device = local_chans // seq_count
    own_rates = lax.dynamic_slice_in_dim(decay_rate, seq_index * per_device, per_device, 1)
    own_residue = lax.dynamic_slice_in_dim(residue, seq_index * per_device, per_device, 1)
    own_skip = lax.dynamic_slice_in_dim(skip_weight, seq_index * per_device, per_device, 0)
    query_part = lax.all_to_all(query, "seq", split_axis=1, concat_axis=2, tiled=True)
    signal_part = lax.all_to_all(product, "seq", split_axis=1, concat_axis=2, tiled=True)
    item_rows = query_part.shape[0]
    start = jnp.zeros((item_rows, modes, per_device), jnp.float32)
    conv, final = local_conv(
        signal_part.astype(jnp.float32), own_rates, own_residue, own_skip, start
    )
    gated = (query_part.astype(jnp.float32) * conv).astype(jnp.bfloat16)
    returned = lax.all_to_all(gated, "seq", split_axis=2, concat_axis=1, tiled=True)
    steps = tokens.shape[1]
    vocab = embedding.shape[0]
    flat_tokens = tokens.reshape(-1)
    one_hot = (flat_tokens[:, None] == jnp.arange(vocab, dtype=jnp.int32)[None, :]).astype(
        jnp.bfloat16
    )
    embedded = jnp.dot(one_hot, embedding, preferred_element_type=jnp.float32)
    partial_sq = jnp.sum(embedded * embedded, axis=1)
    total_sq = lax.psum(partial_sq, "seq")
    normed = (embedded * lax.rsqrt(total_sq / D + 1e-05)[:, None] * norm_gain[None, :]).astype(
        jnp.bfloat16
    )
    proj_terms = jnp.einsum("td,idc->itc", normed, dec_weight, preferred_element_type=jnp.float32)
    projected = lax.psum_scatter(proj_terms, "seq", scatter_dimension=2, tiled=True).astype(
        jnp.bfloat16
    )
    projected = projected.reshape(3, batch_rows, steps, per_device)
    decay = jnp.exp(-own_rates)
    running = final
    outputs = []
    for step in range(steps):
        rounded = lax.optimization_barrier(
            (
                projected[1, :, step].astype(jnp.float32)
                * projected[2, :, step].astype(jnp.float32)
            ).astype(jnp.bfloat16)
        )
        mixed_in = rounded.astype(jnp.float32)
        running = decay[None] * running + mixed_in[:, None, :]
        conv_step = jnp.sum(own_residue[None] * running, axis=1) + own_skip[None] * mixed_in
        outputs.append((projected[0, :, step].astype(jnp.float32) * conv_step).astype(jnp.bfloat16))
    decode_mix = jnp.stack(outputs, axis=1)
    piece = lax.all_gather(decode_mix, "seq", axis=2, tiled=True)
    piece_width = piece.shape[2]
    summed = jnp.dot(piece.reshape(-1, piece_width), out_weight, preferred_element_type=jnp.float32)
    decoded = lax.psum_scatter(summed, "chan", scatter_dimension=1, tiled=True).astype(jnp.bfloat16)
    decoded = decoded.reshape(batch_rows, steps, -1)
    return (returned, decoded)


def solution(mesh):
    placed = (
        P(None, None, "chan", "seq"),
        P(),
        P(),
        P(None, "chan"),
        P(None, "chan"),
        P("chan"),
        P(None, "seq"),
        P("seq"),
        P(None, "seq", "chan"),
        P("chan", "seq"),
    )
    return jax.shard_map(
        body,
        mesh=mesh,
        in_specs=placed,
        out_specs=(P(None, "chan", "seq"), P(None, None, ("seq", "chan"))),
        check_vma=False,
    )
```

profile of v0, /device:TPU:2, one launch (start us, length us, event | category | flops | bytes accessed | tf_op | source)
XLA Modules:
  0.0 975.1 jit_solution(962015850110151932)
XLA Ops:
  7.2 0.0 copy-start
  7.2 0.0 copy-start.5
  7.2 3.5 fusion.69
  10.8 0.7 broadcast_compare_fusion
  11.5 13.2 %fusion.19 = bf16[2,2048,128]{2,0,1:T(2,128)(2,1)} fusion(pred[2,128]{1,0:T(4,128)(4,1)S(1)} %broadcast_compare_fusion, bf16[1,2,2048,128]{3,2,1,0:T(8,128)(2,1)} %get-tuple-element.31, bf16[1,2,2048,128]{3,2,1,0:T(8,128)(2,1)S(1)} %get-tuple-element.30), kind=kLoop, calls=%fused_computation.24 | loop fusion | flops 2621440 | bytes 3145984 | tf_op jit(solution)/shard_map/convert_element_type | solution.py:85
  24.7 9.4 all-to-all-start.1
  34.0 0.8 fusion.68
  34.8 0.1 copy.127
  34.9 0.1 fusion.43
  35.0 0.1 fusion.44
  35.1 0.1 eq.15
  35.2 0.1 copy.126
  35.3 0.3 multiply_reduce_fusion.5
  35.6 0.3 multiply_reduce_fusion
  35.9 0.1 copy.174
  36.0 3.6 copy.213
  39.6 0.1 exponential_multiply_fusion
  39.8 10.8 %all-to-all-done.1 = bf16[2,2048,128]{2,0,1:T(2,128)(2,1)S(1)} async-done(((bf16[2,2048,128]{2,0,1:T(2,128)(2,1)}), bf16[2,2048,128]{2,0,1:T(2,128)(2,1)S(1)}, u32[]{:S(2)}, u32[]{:S(2)}) %all-to-all-start.1) | async-done | bytes 1048608 | tf_op jit(solution)/shard_map/all_to_all | solution.py:91
  50.6 5.7 all-to-all-start
  56.4 141.6 %psum.7 = f32[8]{0:T(128)S(1)} all-reduce(f32[8]{0:T(128)S(1)} %get-tuple-element.52), channel_id=1, replica_groups=mesh['seq'=64,'chan'=4] {'seq'}, use_global_device_ids=true, to_apply=%region_2.3 | all-reduce | flops 8 | bytes 64 | tf_op jit(solution)/shard_map/psum | solution.py:107
  198.0 0.8 dynamic_slice.25
  198.8 0.1 copy.128
  198.9 217.0 %gather_fusion = f32[65536,32]{1,0:T(8,128)} fusion(f32[32,256]{0,1:T(8,128)S(1)} %copy.128, s32[65536]{0:T(1024)S(1)} %broadcast_clamp_fusion), kind=kCustom, calls=%fused_computation | custom fusion | bytes 17039360 | tf_op jit(solution)/shard_map/while/body/eval_jaxpr/jit(_take)/gather | solution.py:25
  415.9 22.2 %copy.129 = f32[256,256,32]{1,0,2:T(8,128)} copy(f32[256,256,32]{2,1,0:T(8,128)} %bitcast.138) | data formatting | bytes 16777216 | tf_op jit(solution)/shard_map/while/body/eval_jaxpr/jit(_take)/gather | solution.py:25
  438.1 0.1 maximum_compare_fusion
  438.2 2.9 copy_bitcast_fusion.1
  441.1 1.6 reshape.199
  442.7 2.2 convolution_bitcast_fusion.1
  444.9 13.7 %fusion.23 = f32[2,16,32,32]{3,0,2,1:T(2,128)S(1)} fusion(f32[32,32]{1,0:T(8,128)S(1)} %fusion.43, f32[16,32]{1,0:T(8,128)S(1)} %get-tuple-element.35, pred[32,32]{1,0:T(8,128)(4,1)S(1)} %fusion.44, f32[2,16,32,32]{3,1,0,2:T(8,128)S(1)} %convolution_bitcast_fusion.1, f32[16,32,32]{2,1,0:T(8,128)S(1)} %exponential_multiply_fusion), kind=kOutput, calls=%fused_computation.28 | convolution fusion | flops 13664256 | bytes 334848 | tf_op jit(solution)/shard_map/while/body/eval_jaxpr/mgnk,bmgk->bmgn/dot_general | solution.py:37
  458.6 8.7 fusion
  467.3 3.8 add_bitcast_fusion
  471.1 7.8 copy.154
  479.0 7.8 copy.132
  486.8 0.0 all-to-all-done
  486.8 3.5 convert_bitcast_fusion
  490.2 11.7 %copy.122 = f32[2,32,64,128]{1,0,3,2:T(2,128)} copy(f32[2,32,64,128]{3,0,1,2:T(2,128)} %convert_bitcast_fusion) | data formatting | bytes 4194304 | tf_op jit(solution)/shard_map/convert_element_type | solution.py:97
  502.0 11.1 %fusion.4 = bf16[2,32,8192]{1,0,2:T(2,128)(2,1)} fusion(f32[2,32,64,128]{1,0,3,2:T(2,128)} %copy.132, f32[2,32,32,256]{1,0,3,2:T(2,128)} %copy.154, f32[2,32,64,128]{1,0,3,2:T(2,128)} %copy.122, f32[32]{0:T(128)S(1)} %dynamic_slice.25), kind=kLoop, calls=%fused_computation.6 | loop fusion | flops 2097152 | bytes 7340160 | tf_op jit(solution)/shard_map/convert_element_type | solution.py:97
  513.1 10.1 %reshape.228 = bf16[64,2,4096]{2,1,0:T(2,128)(2,1)} reshape(bf16[8192,2,32]{2,1,0:T(2,128)(2,1)} %bitcast.141) | data formatting | bytes 2097152
  523.1 10.6 %all-to-all-start.2 = ((bf16[64,2,4096]{2,1,0:T(2,128)(2,1)}), bf16[64,2,4096]{2,1,0:T(2,128)(2,1)S(1)}, u32[]{:S(2)}, u32[]{:S(2)}) async-start(bf16[64,2,4096]{2,1,0:T(2,128)(2,1)} %reshape.228), calls=%async_computation.2 | async-start | bytes 2097152 | tf_op jit(solution)/shard_map/all_to_all | solution.py:98
  533.7 0.0 reduce-scatter.7.cloned.1.call-start
  533.8 0.0 copy-done
  533.8 0.0 copy-done.3
  533.8 0.4 convolution_bitcast_fusion
  534.2 3.0 copy.155
  537.2 5.2 reshape.224
  542.4 0.0 reduce-scatter.7.cloned.1.call-update
  542.5 0.0 reduce-scatter.9.cloned.1.call-start
  542.5 287.7 %reduce-scatter.7.cloned.1.call-done = f32[32,24]{1,0:T(8,128)} async-done(((f32[2048,24]{1,0:T(8,128)}), f32[32,24]{1,0:T(8,128)}) %reduce-scatter.7.cloned.1.call-update) | async-done | bytes 3088
  830.2 0.8 reshape.225
  831.0 0.1 copy.156
  831.2 1.6 slice.73
  832.8 2.0 slice.74
  834.9 0.3 copy.136
  835.1 1.4 copy.137
  836.6 0.1 copy.149
  836.7 90.6 %all_gather.3 = bf16[2,4,2048]{1,0,2:T(2,128)(2,1)} all-gather(bf16[2,4,32]{1,0,2:T(2,128)(2,1)S(1)} %copy.149), channel_id=1, replica_groups=mesh['seq'=64,'chan'=4] {'seq'}, dimensions={2}, use_global_device_ids=true | all-gather | bytes 33280 | tf_op jit(solution)/shard_map/all_gather | solution.py:131
  927.3 2.6 copy.150
  929.9 2.0 convolution_bitcast_fusion.2
  931.9 0.0 reduce-scatter.9.cloned.1.call-update
  931.9 22.0 %reduce-scatter.9.cloned.1.call-done = f32[32,8]{1,0:T(8,128)} async-done(((f32[128,8]{1,0:T(8,128)}), f32[32,8]{1,0:T(8,128)}) %reduce-scatter.9.cloned.1.call-update) | async-done | bytes 1040
  953.9 1.4 copy.158
  955.3 0.0 all-to-all-done.2
  955.3 3.5 reshape.229
  958.8 9.0 copy.134
  (27 shorter events, 0.3 us)
Async XLA Ops:
  7.2 526.6 %copy-start = (bf16[3,128,2048]{2,1,0:T(8,128)(2,1)S(1)}, bf16[3,128,2048]{2,1,0:T(8,128)(2,1)}, u32[]{:S(2)}) copy-start(bf16[3,128,2048]{2,1,0:T(8,128)(2,1)} %param.18) | copy-start | bytes 4718596
  7.2 27.9 %copy-start.5 = (s32[2,4]{1,0:T(2,128)S(1)}, s32[2,4]{1,0:T(2,128)}, u32[]{:S(2)}) copy-start(s32[2,4]{1,0:T(2,128)} %param.12) | copy-start | bytes 100
  7.2 28.1 %copy-start.4 = (bf16[512,128]{1,0:T(8,128)(2,1)S(1)}, bf16[512,128]{1,0:T(8,128)(2,1)}, u32[]{:S(2)}) copy-start(bf16[512,128]{1,0:T(8,128)(2,1)} %param.16) | copy-start | bytes 393220
  24.7 26.0 %all-to-all-start.1 = ((bf16[2,2048,128]{2,0,1:T(2,128)(2,1)}), bf16[2,2048,128]{2,0,1:T(2,128)(2,1)S(1)}, u32[]{:S(2)}, u32[]{:S(2)}) async-start(bf16[2,2048,128]{2,0,1:T(2,128)(2,1)} %fusion.19), calls=%async_computation.1 | async-start | bytes 2097152 | tf_op jit(solution)/shard_map/all_to_all | solution.py:91
  50.6 436.1 %all-to-all-start = ((bf16[2,2048,128]{2,0,1:T(2,128)(2,1)}), bf16[2,2048,128]{2,0,1:T(2,128)(2,1)}, u32[]{:S(2)}, u32[]{:S(2)}) async-start(bf16[2,2048,128]{2,0,1:T(2,128)(2,1)} %bitcast.137), calls=%async_computation | async-start | bytes 2097152 | tf_op jit(solution)/shard_map/all_to_all | solution.py:90
  444.9 13.7 %copy-start.1 = (f32[2,16,32,32]{3,1,0,2:T(8,128)}, f32[2,16,32,32]{3,1,0,2:T(8,128)S(1)}, u32[]{:S(2)}) copy-start(f32[2,16,32,32]{3,1,0,2:T(8,128)S(1)} %convolution_bitcast_fusion.1) | copy-start | bytes 393220
  458.6 8.7 copy-start.2
  502.0 31.9 %copy-start.3 = (f32[128]{0:T(128)S(1)}, f32[128]{0:T(128)}, u32[]{:S(2)}) copy-start(f32[128]{0:T(128)} %param.17) | copy-start | bytes 1540
  523.1 432.1 %all-to-all-start.2 = ((bf16[64,2,4096]{2,1,0:T(2,128)(2,1)}), bf16[64,2,4096]{2,1,0:T(2,128)(2,1)S(1)}, u32[]{:S(2)}, u32[]{:S(2)}) async-start(bf16[64,2,4096]{2,1,0:T(2,128)(2,1)} %reshape.228), calls=%async_computation.2 | async-start | bytes 2097152 | tf_op jit(solution)/shard_map/all_to_all | solution.py:98
  533.7 296.5 %reduce-scatter.7.cloned.1.call-start = ((), (), s32[]{:S(2)}) async-start(), calls=%async_computation.5 | async-start | bytes 1064960
  542.5 411.5 %reduce-scatter.9.cloned.1.call-start = ((), (), s32[]{:S(2)}) async-start(), calls=%async_computation.6 | async-start | bytes 81920
Sparse Core Ops, SparseCore 0:
  542.6 287.5 reduce-scatter.6
  932.0 21.8 reduce-scatter.8
where the time goes:
time: 986 us; the launch traced here: 975 us
  waiting for transfers between devices  321 us (33%)
  local copies, waits for them, and re-layouts  318 us (32%)
  blocking collectives  232 us (24%)
  other arithmetic  33 us (3%)
  matrix products  31.1 us (3%)
  starting transfers between devices  25.8 us (3%)
  between operations  14.8 us (2%)
    unnamed x4, waiting for transfers between devices  310 us
    gather x2, local copies, waits for them, and re-layouts, one_group(): jnp.take(filt, jnp.maximum(distance, 0), axis=1)  239 us
    psum x1, blocking collectives, body(): total_sq = lax.psum(partial_sq, 'seq')  142 us
    all_gather x1, blocking collectives, body(): piece = lax.all_gather(decode_mix, 'seq', axis=2, tiled=True)  90.6 us
    unnamed x21, local copies, waits for them, and re-layouts  27.9 us
  transfers between devices with their start and end apart: 5, of which 3 were waited for; matrix products, arithmetic and copies ran while one was open for 32% of the time, Pallas kernels for 0%

commit v1 on v0

--- a/solution.py
+++ b/solution.py
@@ -1,3 +1,4 @@
+import functools
 import math
 import jax
 import jax.numpy as jnp
@@ -6,6 +7,16 @@
 
 D = 8192
 highest = lax.Precision.HIGHEST
+
+
+def cover_quarters(mine_x, at_axis):
+    piece_next = lax.axis_size("seq")
+    p_next = lax.all_to_all(jnp.stack([mine_x] * piece_next, axis=0), "seq", 0, 0)
+    front = jnp.concatenate(p_next, axis=at_axis)
+    return front
+
+
+lay_cycles = functools.partial(cover_quarters, at_axis=2)
 
 
 def local_conv(signal, rates, residues, skips, start_state):
@@ -128,7 +139,7 @@
         conv_step = jnp.sum(own_residue[None] * running, axis=1) + own_skip[None] * mixed_in
         outputs.append((projected[0, :, step].astype(jnp.float32) * conv_step).astype(jnp.bfloat16))
     decode_mix = jnp.stack(outputs, axis=1)
-    piece = lax.all_gather(decode_mix, "seq", axis=2, tiled=True)
+    piece = lay_cycles(decode_mix)
     piece_width = piece.shape[2]
     summed = jnp.dot(piece.reshape(-1, piece_width), out_weight, preferred_element_type=jnp.float32)
     decoded = lax.psum_scatter(summed, "chan", scatter_dimension=1, tiled=True).astype(jnp.bfloat16)

time: 986 us -> 650 us (0.66)
  waiting for transfers between devices: 321 us -> 65.2 us
  blocking collectives: 232 us -> 141 us
  starting transfers between devices: 25.8 us -> 37.9 us
    unnamed x4, waiting for transfers between devices: 310 us -> 65.2 us
    all_gather x1 -> x0, blocking collectives: 90.6 us -> none  [body(): piece = lax.all_gather(decode_mix, 'seq', axis=2, tiled=True)]
    all_to_all x1, waiting for transfers between devices: 10.8 us -> 0.01 us  [body(): lax.all_to_all(product, 'seq', split_axis=1, concat_axis=2, tiled=True)]
    unnamed x21 -> x31, local copies, waits for them, and re-layouts: 27.9 us -> 36.3 us
  transfers between devices with their start and end apart: 5 -> 6, of which waited for: 3 -> 2; matrix products, arithmetic and copies ran while one was open for 32% -> 55% of each run, Pallas kernels for 0% -> 0%
where the time goes in v1:
time: 650 us; the launch traced here: 642 us
  local copies, waits for them, and re-layouts  320 us (49%)
  blocking collectives  141 us (22%)
  waiting for transfers between devices  65.2 us (10%)
  starting transfers between devices  37.9 us (6%)
  other arithmetic  33 us (5%)
  matrix products  30 us (5%)
  between operations  14.5 us (2%)
    gather x2, local copies, waits for them, and re-layouts, one_group(): jnp.take(filt, jnp.maximum(distance, 0), axis=1)  239 us
    psum x1, blocking collectives, body(): total_sq = lax.psum(partial_sq, 'seq')  141 us
    unnamed x4, waiting for transfers between devices  65.2 us
    unnamed x31, local copies, waits for them, and re-layouts  36.3 us
    dot_general x1, matrix products, one_group(): jnp.einsum('mgnk,bmgk->bmgn', spread, block_sums, precision=highest)  13.9 us
    convert_element_type x2, other arithmetic, body(): gated = (query_part.astype(jnp.float32) * conv).astype(jnp.bfloat16)  13.4 us
    convert_element_type x1, other arithmetic, body(): product = jnp.where(live[:, None, :], keys_in.astype(jnp.float32) * value...  13.2 us
  transfers between devices with their start and end apart: 6, of which 2 were waited for; matrix products, arithmetic and copies ran while one was open for 55% of the time, Pallas kernels for 0%

profile of v1, /device:TPU:2, one launch (start us, length us, event | category | flops | bytes accessed | tf_op | source)
XLA Modules:
  0.0 642.1 jit_solution(967754967729831648)
XLA Ops:
  7.2 0.0 copy-start
  7.2 3.5 fusion.69
  10.7 0.7 broadcast_compare_fusion
  11.4 13.2 %fusion.19 = bf16[2,2048,128]{2,0,1:T(2,128)(2,1)} fusion(pred[2,128]{1,0:T(4,128)(4,1)S(1)} %broadcast_compare_fusion, bf16[1,2,2048,128]{3,2,1,0:T(8,128)(2,1)} %get-tuple-element.31, bf16[1,2,2048,128]{3,2,1,0:T(8,128)(2,1)S(1)} %get-tuple-element.30), kind=kLoop, calls=%fused_computation.24 | loop fusion | flops 2621440 | bytes 3145984 | tf_op jit(solution)/shard_map/convert_element_type | solution.py:96
  24.6 9.4 %all-to-all-start.1 = ((bf16[2,2048,128]{2,0,1:T(2,128)(2,1)}), bf16[2,2048,128]{2,0,1:T(2,128)(2,1)S(1)}, u32[]{:S(2)}, u32[]{:S(2)}) async-start(bf16[2,2048,128]{2,0,1:T(2,128)(2,1)} %fusion.19), calls=%async_computation.1 | async-start | bytes 2097152 | tf_op jit(solution)/shard_map/all_to_all | solution.py:102
  34.0 0.0 reduce-scatter.7.cloned.1.call-start
  34.1 0.1 eq.15
  34.2 0.3 multiply_reduce_fusion.5
  34.5 141.4 %psum.7 = f32[8]{0:T(128)S(1)} all-reduce(f32[8]{0:T(128)S(1)} %get-tuple-element.52), channel_id=1, replica_groups=mesh['seq'=64,'chan'=4] {'seq'}, use_global_device_ids=true, to_apply=%region_2.3 | all-reduce | flops 8 | bytes 64 | tf_op jit(solution)/shard_map/psum | solution.py:118
  175.9 0.4 convolution_bitcast_fusion
  176.2 3.1 copy.156
  179.3 5.3 reshape.226
  184.5 0.0 reduce-scatter.7.cloned.1.call-update
  184.6 0.1 copy.175
  184.8 0.8 fusion.68
  185.6 0.1 copy.128
  185.7 0.1 copy.127
  185.8 0.3 multiply_reduce_fusion
  186.0 0.1 fusion.44
  186.1 0.1 fusion.43
  186.2 0.8 dynamic_slice.25
  186.9 0.1 copy.129
  187.0 217.0 %gather_fusion = f32[65536,32]{1,0:T(8,128)} fusion(f32[32,256]{0,1:T(8,128)S(1)} %copy.129, s32[65536]{0:T(1024)S(1)} %broadcast_clamp_fusion), kind=kCustom, calls=%fused_computation | custom fusion | bytes 17039360 | tf_op jit(solution)/shard_map/while/body/eval_jaxpr/jit(_take)/gather | solution.py:36
  404.1 22.4 %copy.130 = f32[256,256,32]{1,0,2:T(8,128)} copy(f32[256,256,32]{2,1,0:T(8,128)} %bitcast.141) | data formatting | bytes 16777216 | tf_op jit(solution)/shard_map/while/body/eval_jaxpr/jit(_take)/gather | solution.py:36
  426.4 9.4 %copy.214 = bf16[1,2,2048,128]{3,1,2,0:T(2,128)(2,1)} copy(bf16[1,2,2048,128]{3,2,1,0:T(8,128)(2,1)S(1)} %copy-done.3) | data formatting | bytes 2097152
  435.9 0.1 maximum_compare_fusion
  436.0 0.1 exponential_multiply_fusion
  436.1 37.3 %reduce-scatter.7.cloned.1.call-done = f32[32,24]{1,0:T(8,128)} async-done(((f32[2048,24]{1,0:T(8,128)}), f32[32,24]{1,0:T(8,128)}) %reduce-scatter.7.cloned.1.call-update) | async-done | bytes 3088
  473.4 0.8 reshape.227
  474.2 0.1 copy.157
  474.4 0.0 all-to-all-done.1
  474.4 0.0 copy-start.2
  474.4 1.0 copy-done.2
  475.4 10.6 %all-to-all-start = ((bf16[2,2048,128]{2,0,1:T(2,128)(2,1)}), bf16[2,2048,128]{2,0,1:T(2,128)(2,1)S(1)}, u32[]{:S(2)}, u32[]{:S(2)}) async-start(bf16[2,2048,128]{2,0,1:T(2,128)(2,1)} %bitcast.140), calls=%async_computation | async-start | bytes 2097152 | tf_op jit(solution)/shard_map/all_to_all | solution.py:101
  486.0 4.1 copy_bitcast_fusion.1
  490.1 1.6 reshape.201
  491.7 2.2 convolution_bitcast_fusion.1
  493.9 0.2 slice.74
  494.1 13.9 %fusion.23 = f32[2,16,32,32]{3,0,2,1:T(2,128)S(1)} fusion(f32[32,32]{1,0:T(8,128)S(1)} %fusion.43, f32[16,32]{1,0:T(8,128)S(1)} %get-tuple-element.35, pred[32,32]{1,0:T(8,128)(4,1)S(1)} %fusion.44, f32[2,16,32,32]{3,1,0,2:T(8,128)S(1)} %convolution_bitcast_fusion.1, f32[16,32,32]{2,1,0:T(8,128)S(1)} %exponential_multiply_fusion), kind=kOutput, calls=%fused_computation.28 | convolution fusion | flops 13664256 | bytes 334848 | tf_op jit(solution)/shard_map/while/body/eval_jaxpr/mgnk,bmgk->bmgn/dot_general | solution.py:48
  508.0 0.8 copy-done.4
  508.8 0.6 slice.73
  509.4 0.3 copy.137
  509.6 0.4 copy.138
  510.1 0.7 reshape.232
  510.9 8.5 %fusion = f32[32,2,32,256]{3,2,1,0:T(8,128)S(1)} fusion(bf16[2,32,32,256]{3,2,0,1:T(8,128)(2,1)S(1)} %reshape.201, f32[256,256,32]{1,0,2:T(8,128)} %copy.130, pred[256,256]{1,0:T(8,128)(4,1)S(1)} %get-tuple-element.56, pred[256,256]{1,0:T(8,128)(4,1)S(1)} %get-tuple-element.55), kind=kOutput, calls=%fused_computation.1 | convolution fusion | flops 1614807040 | bytes 11665408 | tf_op jit(solution)/shard_map/while/body/eval_jaxpr/gij,bgnj->bgni/dot_general | solution.py:38
  519.4 3.8 add_bitcast_fusion
  523.2 7.8 %copy.155 = f32[2,32,32,256]{1,0,3,2:T(2,128)} copy(f32[2,32,32,256]{3,2,0,1:T(8,128)} %add_bitcast_fusion) | data formatting | bytes 4194304 | tf_op jit(solution)/shard_map/while/body/eval_jaxpr/reshape | solution.py:54
  531.0 7.8 %copy.133 = f32[2,32,64,128]{1,0,3,2:T(2,128)} copy(f32[2,32,64,128]{3,2,0,1:T(8,128)} %get-tuple-element.33) | data formatting | bytes 4194304 | tf_op jit(solution)/shard_map/convert_element_type | solution.py:106
  538.9 9.0 %all-to-all-start.3 = ((bf16[64,2,128]{2,1,0:T(2,128)(2,1)}), bf16[64,2,128]{2,1,0:T(2,128)(2,1)S(1)}, u32[]{:S(2)}, u32[]{:S(2)}) async-start(bf16[64,2,128]{2,1,0:T(2,128)(2,1)} %reshape.232), calls=%async_computation.3 | async-start | bytes 65536 | tf_op jit(solution)/shard_map/all_to_all | solution.py:14
  547.9 2.2 convert_bitcast_fusion
  550.1 11.8 %copy.123 = f32[2,32,64,128]{1,0,3,2:T(2,128)} copy(f32[2,32,64,128]{3,0,1,2:T(2,128)} %convert_bitcast_fusion) | data formatting | bytes 4194304 | tf_op jit(solution)/shard_map/convert_element_type | solution.py:108
  561.9 11.2 %fusion.4 = bf16[2,32,8192]{1,0,2:T(2,128)(2,1)} fusion(f32[2,32,64,128]{1,0,3,2:T(2,128)} %copy.133, f32[2,32,32,256]{1,0,3,2:T(2,128)} %copy.155, f32[2,32,64,128]{1,0,3,2:T(2,128)} %copy.123, f32[32]{0:T(128)S(1)} %dynamic_slice.25), kind=kLoop, calls=%fused_computation.6 | loop fusion | flops 2097152 | bytes 7340160 | tf_op jit(solution)/shard_map/convert_element_type | solution.py:108
  573.0 10.0 %reshape.230 = bf16[64,2,4096]{2,1,0:T(2,128)(2,1)} reshape(bf16[8192,2,32]{2,1,0:T(2,128)(2,1)} %bitcast.144) | data formatting | bytes 2097152
  583.0 8.9 %all-to-all-start.2 = ((bf16[64,2,4096]{2,1,0:T(2,128)(2,1)}), bf16[64,2,4096]{2,1,0:T(2,128)(2,1)S(1)}, u32[]{:S(2)}, u32[]{:S(2)}) async-start(bf16[64,2,4096]{2,1,0:T(2,128)(2,1)} %reshape.230), calls=%async_computation.2 | async-start | bytes 2097152 | tf_op jit(solution)/shard_map/all_to_all | solution.py:109
  591.9 0.0 reduce-scatter.9.cloned.1.call-start
  592.0 0.1 reshape.233
  592.1 0.2 reshape_reshape.3
  592.3 1.0 convolution_bitcast_fusion.2
  593.3 0.0 reduce-scatter.9.cloned.1.call-update
  593.3 27.8 %reduce-scatter.9.cloned.1.call-done = f32[32,8]{1,0:T(8,128)} async-done(((f32[128,8]{1,0:T(8,128)}), f32[32,8]{1,0:T(8,128)}) %reduce-scatter.9.cloned.1.call-update) | async-done | bytes 1040
  621.1 1.4 copy.159
  622.5 0.0 all-to-all-done.2
  622.5 3.5 reshape.231
  626.0 9.0 %copy.135 = bf16[2,64,32,128]{3,2,1,0:T(8,128)(2,1)} copy(bf16[2,64,32,128]{2,0,3,1:T(2,128)(2,1)} %bitcast.142) | data formatting | bytes 2097152 | tf_op jit(solution)/shard_map/all_to_all | solution.py:109
  (39 shorter events, 0.3 us)
Async XLA Ops:
  7.2 168.7 %copy-start = (bf16[3,128,2048]{2,1,0:T(8,128)(2,1)S(1)}, bf16[3,128,2048]{2,1,0:T(8,128)(2,1)}, u32[]{:S(2)}) copy-start(bf16[3,128,2048]{2,1,0:T(8,128)(2,1)} %param.18) | copy-start | bytes 4718596
  7.2 26.9 %copy-start.9 = (s32[2,4]{1,0:T(2,128)S(1)}, s32[2,4]{1,0:T(2,128)}, u32[]{:S(2)}) copy-start(s32[2,4]{1,0:T(2,128)} %param.12) | copy-start | bytes 100
  7.2 27.0 %copy-start.8 = (bf16[512,128]{1,0:T(8,128)(2,1)S(1)}, bf16[512,128]{1,0:T(8,128)(2,1)}, u32[]{:S(2)}) copy-start(bf16[512,128]{1,0:T(8,128)(2,1)} %param.16) | copy-start | bytes 393220
  7.2 168.7 %copy-start.7 = (f32[128]{0:T(128)S(1)}, f32[128]{0:T(128)}, u32[]{:S(2)}) copy-start(f32[128]{0:T(128)} %param.17) | copy-start | bytes 1540
  24.6 449.8 %all-to-all-start.1 = ((bf16[2,2048,128]{2,0,1:T(2,128)(2,1)}), bf16[2,2048,128]{2,0,1:T(2,128)(2,1)S(1)}, u32[]{:S(2)}, u32[]{:S(2)}) async-start(bf16[2,2048,128]{2,0,1:T(2,128)(2,1)} %fusion.19), calls=%async_computation.1 | async-start | bytes 2097152 | tf_op jit(solution)/shard_map/all_to_all | solution.py:102
  34.0 439.4 %reduce-scatter.7.cloned.1.call-start = ((), (), s32[]{:S(2)}) async-start(), calls=%async_computation.6 | async-start | bytes 1064960
  404.1 22.4 %copy-start.3 = (bf16[1,2,2048,128]{3,2,1,0:T(8,128)(2,1)S(1)}, bf16[1,2,2048,128]{3,2,1,0:T(8,128)(2,1)}, u32[]{:S(2)}) copy-start(bf16[1,2,2048,128]{3,2,1,0:T(8,128)(2,1)} %get-tuple-element.29) | copy-start | bytes 3145732
  474.4 1.0 copy-start.2
  475.4 63.5 %all-to-all-start = ((bf16[2,2048,128]{2,0,1:T(2,128)(2,1)}), bf16[2,2048,128]{2,0,1:T(2,128)(2,1)S(1)}, u32[]{:S(2)}, u32[]{:S(2)}) async-start(bf16[2,2048,128]{2,0,1:T(2,128)(2,1)} %bitcast.140), calls=%async_computation | async-start | bytes 2097152 | tf_op jit(solution)/shard_map/all_to_all | solution.py:101
  508.0 0.8 copy-start.4
  509.6 9.8 %copy-start.5 = (f32[2,16,32,32]{3,0,2,1:T(2,128)S(1)}, f32[2,16,32,32]{3,0,2,1:T(2,128)}, u32[]{:S(2)}) copy-start(f32[2,16,32,32]{3,0,2,1:T(2,128)} %copy-done.4) | copy-start | bytes 393220
  538.9 44.1 %all-to-all-start.3 = ((bf16[64,2,128]{2,1,0:T(2,128)(2,1)}), bf16[64,2,128]{2,1,0:T(2,128)(2,1)S(1)}, u32[]{:S(2)}, u32[]{:S(2)}) async-start(bf16[64,2,128]{2,1,0:T(2,128)(2,1)} %reshape.232), calls=%async_computation.3 | async-start | bytes 65536 | tf_op jit(solution)/shard_map/all_to_all | solution.py:14
  561.9 30.4 %copy-start.6 = (bf16[2048,128]{1,0:T(8,128)(2,1)S(1)}, bf16[2048,128]{1,0:T(8,128)(2,1)}, u32[]{:S(2)}) copy-start(bf16[2048,128]{1,0:T(8,128)(2,1)} %param.19) | copy-start | bytes 1572868
  573.0 62.0 %copy-start.1 = (bf16[3,128,2048]{2,1,0:T(8,128)(2,1)S(1)}, bf16[3,128,2048]{2,1,0:T(8,128)(2,1)}, u32[]{:S(2)}) copy-start(bf16[3,128,2048]{2,1,0:T(8,128)(2,1)} %param.18) | copy-start | bytes 4718596
  583.0 39.5 %all-to-all-start.2 = ((bf16[64,2,4096]{2,1,0:T(2,128)(2,1)}), bf16[64,2,4096]{2,1,0:T(2,128)(2,1)S(1)}, u32[]{:S(2)}, u32[]{:S(2)}) async-start(bf16[64,2,4096]{2,1,0:T(2,128)(2,1)} %reshape.230), calls=%async_computation.2 | async-start | bytes 2097152 | tf_op jit(solution)/shard_map/all_to_all | solution.py:109
  591.9 29.2 %reduce-scatter.9.cloned.1.call-start = ((), (), s32[]{:S(2)}) async-start(), calls=%async_computation.7 | async-start | bytes 81920
Sparse Core Ops, SparseCore 0:
  184.7 288.6 reduce-scatter.6
  595.2 25.8 reduce-scatter.8
